TPU v7x, 32 devices: a whole 2x2x4 slice. The times are simulated.
32 devices in a mesh: groups: 2 (over y), seq: 4 (over z), tensor: 4 (over x, core).
Axes of the slice: x: 2, y: 2, z: 4, core: 2. Of those that a mesh axis runs over, the one named last changes fastest.
Arguments:
- activations: bfloat16 [2048, 4096], P(('groups', 'seq')), parts along dimension 0, may hold values from -6 to 6
- token_adapter_index: int32 [2048], P(('groups', 'seq')), parts along dimension 0, may hold values from 0 to 15
- gate_scanned_weight: bfloat16 [4096, 2, 8192], P('seq', None, 'tensor'), may hold values from -0.09375 to 0.09375
- state_vector_weight: bfloat16 [4096, 2, 1024], P('seq'), may hold values from -0.09375 to 0.09375
- time_step_weight: bfloat16 [4096, 128], P('seq', 'tensor'), may hold values from -0.09375 to 0.09375
- adapter_down_maps: bfloat16 [4096, 256], P('seq'), may hold values from -0.09375 to 0.09375
- adapter_up_maps: bfloat16 [256, 2, 8192], P(None, None, 'tensor'), may hold values from -1.5 to 1.5
- scanned_channel_taps: float32 [4, 8192], P(None, 'tensor'), may hold values from -3 to 3
- state_vector_taps: float32 [4, 2, 1024], replicated, may hold values from -3 to 3
- earlier_scanned_channels: bfloat16 [6, 8192], P('groups', 'tensor'), parts along dimension 0, may hold values from -6 to 6
- earlier_state_vectors: bfloat16 [6, 2, 1024], P('groups'), parts along dimension 0, may hold values from -6 to 6
- head_step_bias: float32 [128], P('tensor'), may hold values from -4 to -1
- adapter_step_shift: float32 [16, 128], P(None, 'tensor'), may hold values from -3 to 3
- head_decay_rate: float32 [128], P('tensor'), may hold values from 0.0001953125 to 0.3
- starting_head_state: float32 [256, 64, 128], P(('groups', 'tensor')), parts along dimension 0, may hold values from -6 to 6
- gated_norm_gain: float32 [8192], P('tensor'), may hold values from 0.1 to 1.9
- output_projection_weight: bfloat16 [8192, 4096], P('tensor', 'seq'), may hold values from -0.0625 to 0.0625
Outputs:
- mixed: bfloat16 [2048, 4096], P(('groups', 'tensor'), 'seq'), parts along dimension 0
- checkpoints: float32 [8, 128, 64, 128], P(('groups', 'seq'), 'tensor'), parts along dimension 0
There are 2 independent parts, one for each index of `groups`. A program takes and returns all parts, laid end to end along the dimension named above; an argument that names none is the same for every part. Nothing has to cross between parts.
All inputs are finite; a program needn't handle non-finite values.
Results may differ from a plain program's by a relative error of at most 0.02.
Values may be sent and summed in bfloat16 or wider, within the bound.
No kernel may reach another device: no remote copies, remote signals or barrier semaphores. Data moves between devices by JAX's collectives and lax.ppermute only.
A program may use at most 192 MiB of HBM per device.

v0:
```python
import jax
import jax.numpy as jnp
from jax import lax
from jax.sharding import PartitionSpec as P

HEADS = 128
HEAD_DIM = 64
STATE = 128
HEAD_SETS = 8
ADAPTER_COUNT = 16
ADAPTER_RANK = 16
CONV = 4
BLOCK = 128


def passed_along(array, axis, by):
    peers = lax.axis_size(axis)
    pairs = [(i, i + by) for i in range(peers) if 0 <= i + by < peers]
    return lax.ppermute(array, axis, pairs)


def entering_2(array, axis, join, neutral):
    place = lax.axis_index(axis)
    gathered = jax.tree.map(
        lambda a, kind: lax.all_gather(a.astype(kind), axis),
        array,
        jax.tree.map(lambda a: jnp.bfloat16 if a.dtype == jnp.float32 else a.dtype, array),
    )
    state = jax.tree.map(lambda a, e: jnp.zeros_like(a) + jnp.asarray(e, a.dtype), array, neutral)

    def one(lap, state):
        return join(
            state,
            jax.tree.map(
                lambda a, own: lax.dynamic_index_in_dim(a, lap, 0, False).astype(own.dtype),
                gathered,
                array,
            ),
        )

    return lax.fori_loop(0, place, one, state)


def settle(value):
    return lax.optimization_barrier(value.astype(jnp.bfloat16))


def causal_conv(series, prior, kernel):
    count = series.shape[0]
    padded = jnp.concatenate([prior, series], axis=0).astype(jnp.float32)
    total = jnp.zeros(series.shape, jnp.float32)
    for offset in range(CONV):
        total = total + kernel[offset] * padded[offset : offset + count]
    return settle(jax.nn.silu(total))


def join_states(earlier, later):
    return (earlier[0] + later[0], jnp.exp(later[0])[:, None, None] * earlier[1] + later[1])


def per_device(
    activations,
    token_adapter_index,
    gate_scanned_weight,
    state_vector_weight,
    time_step_weight,
    adapter_down_maps,
    adapter_up_maps,
    scanned_channel_taps,
    state_vector_taps,
    earlier_scanned_channels,
    earlier_state_vectors,
    head_step_bias,
    adapter_step_shift,
    head_decay_rate,
    starting_head_state,
    gated_norm_gain,
    output_projection_weight,
):
    tokens_here = activations.shape[0]
    heads_here = time_step_weight.shape[1]
    local_inner_channels = gate_scanned_weight.shape[2]
    per_set = HEADS // HEAD_SETS
    sets_here = max(1, heads_here // per_set)
    heads_per = heads_here // sets_here
    first_set = lax.axis_index("tensor") * heads_here // per_set
    io_start = first_set * STATE
    io_width = sets_here * STATE
    mine_io = lax.dynamic_slice_in_dim(state_vector_weight, io_start, io_width, 2)
    kernel_io = lax.dynamic_slice_in_dim(state_vector_taps, io_start, io_width, 2).reshape(
        CONV, 2 * io_width
    )
    prior_io = lax.dynamic_slice_in_dim(earlier_state_vectors, io_start, io_width, 2).reshape(
        CONV - 1, 2 * io_width
    )
    owner_adapter = jnp.arange(ADAPTER_COUNT * ADAPTER_RANK, dtype=jnp.int32) // ADAPTER_RANK
    chosen = token_adapter_index[:, None] == owner_adapter[None, :]
    chosen_up_weight = adapter_up_maps.reshape(
        ADAPTER_COUNT * ADAPTER_RANK, 2 * local_inner_channels
    )

    def add_product(piece):
        return jnp.dot(
            activations, piece.reshape(piece.shape[0], -1), preferred_element_type=jnp.float32
        )

    pieces = (
        lax.all_gather(gate_scanned_weight, "seq", axis=0, tiled=True),
        lax.all_gather(mine_io, "seq", axis=0, tiled=True),
        lax.all_gather(time_step_weight, "seq", axis=0, tiled=True),
        lax.all_gather(adapter_down_maps, "seq", axis=0, tiled=True),
    )
    pair_raw, io_raw, step_raw, adapter_hidden = tuple(
        (add_product(pieces[index]) for index in range(len(pieces)))
    )
    adapter_hidden = settle(jnp.where(chosen, adapter_hidden, 0.0))
    pair_raw = pair_raw + jnp.dot(
        adapter_hidden, chosen_up_weight, preferred_element_type=jnp.float32
    )
    gate_and_scanned = settle(pair_raw).reshape(tokens_here, 2, local_inner_channels)
    gate_values = gate_and_scanned[:, 0]
    mix_values = gate_and_scanned[:, 1]
    state_io = settle(io_raw)
    rim_rows = passed_along(
        (mix_values[tokens_here - (CONV - 1) :], state_io[tokens_here - (CONV - 1) :]), "seq", 1
    )
    at_start = lax.axis_index("seq") == 0
    rim_mix = jnp.where(at_start, earlier_scanned_channels, rim_rows[0])
    rim_io = jnp.where(at_start, prior_io, rim_rows[1])
    mix_conv = causal_conv(mix_values, rim_mix, scanned_channel_taps)
    state_conv = causal_conv(state_io, rim_io, kernel_io).reshape(tokens_here, 2, sets_here, STATE)
    onehot = (
        token_adapter_index[:, None] == jnp.arange(ADAPTER_COUNT, dtype=jnp.int32)[None, :]
    ).astype(jnp.float32)
    shift_here = jnp.dot(
        onehot,
        adapter_step_shift,
        precision=lax.Precision.HIGHEST,
        preferred_element_type=jnp.float32,
    )
    timestep = jax.nn.softplus(step_raw + head_step_bias + shift_here)
    blocks = tokens_here // BLOCK
    mix_blocks = mix_conv.reshape(blocks, BLOCK, heads_here, HEAD_DIM)
    input_blocks = state_conv[:, 0].reshape(blocks, BLOCK, sets_here, STATE)
    output_blocks = state_conv[:, 1].reshape(blocks, BLOCK, sets_here, STATE)
    step_blocks = timestep.reshape(blocks, BLOCK, heads_here)
    cumulative = jnp.cumsum(-head_decay_rate * step_blocks, axis=1)
    scores = jnp.einsum(
        "bign,bjgn->bgij", output_blocks, input_blocks, preferred_element_type=jnp.float32
    )
    scores = jnp.repeat(scores, heads_per, axis=1)
    cum_heads = jnp.swapaxes(cumulative, 1, 2)
    gaps = cum_heads[:, :, :, None] - cum_heads[:, :, None, :]
    row_index = lax.broadcasted_iota(jnp.int32, (BLOCK, BLOCK), 0)
    col_index = lax.broadcasted_iota(jnp.int32, (BLOCK, BLOCK), 1)
    causal = row_index >= col_index
    weight = jnp.where(causal, jnp.exp(jnp.minimum(gaps, 0.0)), 0.0)
    mixing = settle(scores * weight * jnp.swapaxes(step_blocks, 1, 2)[:, :, None, :])
    intra_out = jnp.einsum(
        "bhij,bjhp->bihp", mixing, mix_blocks, preferred_element_type=jnp.float32
    )
    input_heads = jnp.repeat(input_blocks, heads_per, axis=2)
    output_heads = jnp.repeat(output_blocks, heads_per, axis=2)
    block_total = cumulative[:, -1]
    scaled = settle(
        mix_blocks.astype(jnp.float32)
        * (step_blocks * jnp.exp(block_total[:, None, :] - cumulative))[..., None]
    )
    update = jnp.einsum("bjhp,bjhn->bhpn", scaled, input_heads, preferred_element_type=jnp.float32)
    empty_decay = jnp.zeros((heads_here,), jnp.float32)
    empty_state = jnp.zeros((heads_here, HEAD_DIM, STATE), jnp.float32)
    carried = (empty_decay, empty_state)
    prefix_decay = []
    prefix_state = []
    for block in range(blocks):
        prefix_decay.append(carried[0])
        prefix_state.append(carried[1])
        carried = join_states(carried, (block_total[block], update[block]))
    before = entering_2(carried, "seq", join_states, (empty_decay, empty_state))
    entering = jnp.exp(before[0])[:, None, None] * starting_head_state + before[1]
    block_states = jnp.exp(jnp.stack(prefix_decay))[:, :, None, None] * entering[None] + jnp.stack(
        prefix_state
    )
    inter_out = jnp.exp(cumulative)[..., None] * jnp.einsum(
        "bihn,bhpn->bihp",
        output_heads.astype(jnp.float32),
        block_states,
        precision=lax.Precision.HIGHEST,
    )
    finish = jnp.exp(carried[0])[:, None, None] * entering + carried[1]
    scan_out = (intra_out + inter_out).reshape(tokens_here, local_inner_channels)
    gated = settle(scan_out * jax.nn.silu(gate_values.astype(jnp.float32)))
    gathered = lax.all_gather(gated, "seq", axis=0, tiled=True)
    squares = jnp.sum(jnp.square(gathered.astype(jnp.float32)), axis=1)
    hidden = settle(gathered.astype(jnp.float32) * gated_norm_gain)
    partial_sum = jnp.dot(hidden, output_projection_weight, preferred_element_type=jnp.float32)
    summed, total_squares = (
        lax.psum_scatter(
            partial_sum.astype(jnp.bfloat16), "tensor", scatter_dimension=0, tiled=True
        ).astype(jnp.float32),
        lax.psum_scatter(
            squares.astype(jnp.bfloat16), "tensor", scatter_dimension=0, tiled=True
        ).astype(jnp.float32),
    )
    mixed = (summed * lax.rsqrt(total_squares / (HEADS * HEAD_DIM) + 1e-05)[:, None]).astype(
        jnp.bfloat16
    )
    return (mixed, finish[None])


def solution(mesh):
    return jax.shard_map(
        per_device,
        mesh=mesh,
        in_specs=(
            P(("groups", "seq"), None),
            P(("groups", "seq")),
            P("seq", None, "tensor"),
            P("seq", None, None),
            P("seq", "tensor"),
            P("seq", None),
            P(None, None, "tensor"),
            P(None, "tensor"),
            P(),
            P("groups", "tensor"),
            P("groups", None, None),
            P("tensor"),
            P(None, "tensor"),
            P("tensor"),
            P(("groups", "tensor"), None, None),
            P("tensor"),
            P("tensor", "seq"),
        ),
        out_specs=(P(("groups", "tensor"), "seq"), P(("groups", "seq"), "tensor", None, None)),
        check_vma=False,
    )
```

profile of v0, /device:TPU:0, one launch (start us, length us, event | category | flops | bytes accessed | tf_op | source)
XLA Modules:
  0.0 960.9 jit_solution(7413483118449499834)
XLA Ops:
  7.2 3.1 constant_dynamic-slice_fusion.1
  13.6 17.2 %all_gather.26 = bf16[4096,32]{0,1:T(8,128)(2,1)S(1)} all-gather(bf16[1024,32]{0,1:T(8,128)(2,1)S(1)} %copy-done.14), channel_id=1, replica_groups=mesh['groups'=2,'seq'=4,'tensor'=4] {'seq'}, dimensions={0}, use_global_device_ids=true | all-gather | bytes 327680 | tf_op jit(solution)/shard_map/all_gather | solution.py:110
  34.5 3.9 copy.76
  39.6 56.1 %all-gather.11.cloned.1.call-done = bf16[4096,2,256]{2,1,0:T(2,128)(2,1)} async-done(((bf16[1024,2,256]{2,1,0:T(2,128)(2,1)}), bf16[4096,2,256]{2,1,0:T(2,128)(2,1)}) %all-gather.11.cloned.1.call-update) | async-done | bytes 4194320 | tf_op jit(solution)/shard_map/all_gather | solution.py:109
  95.7 2.9 copy.78
  101.5 40.3 %all-gather.9.cloned.1.call-done = bf16[4096,256]{1,0:T(8,128)(2,1)} async-done(((bf16[1024,256]{1,0:T(8,128)(2,1)}), bf16[4096,256]{1,0:T(8,128)(2,1)}) %all-gather.9.cloned.1.call-update) | async-done | bytes 2097168 | tf_op jit(solution)/shard_map/all_gather | solution.py:111
  141.8 3.0 fusion.17
  146.5 557.4 %all-gather.7.cloned.1.call-done = bf16[4096,2,2048]{2,1,0:T(2,128)(2,1)} async-done(((bf16[1024,2,2048]{2,1,0:T(2,128)(2,1)}), bf16[4096,2,2048]{2,1,0:T(2,128)(2,1)}) %all-gather.7.cloned.1.call-update) | async-done | bytes 33554448 | tf_op jit(solution)/shard_map/all_gather | solution.py:108
  703.9 23.2 %copy.75 = bf16[512,8,2,2048]{3,1,2,0:T(8,128)(2,1)} copy(bf16[512,8,2,2048]{3,2,1,0:T(2,128)(2,1)} %bitcast.126) | data formatting | bytes 67108864
  727.1 15.2 %fusion.39 = f32[256,4096]{1,0:T(8,128)S(1)} fusion(bf16[256,4096]{1,0:T(8,128)(2,1)S(1)} %copy-done, bf16[4096,4096]{1,0:T(8,128)(2,1)} %bitcast.127), kind=kOutput, calls=%fused_computation.102 | convolution fusion | flops 8589934592 | bytes 39845888 | tf_op jit(solution)/shard_map/dot_general | solution.py:103
  742.3 2.1 fusion.2
  744.4 3.3 copy.71
  749.3 11.5 %collective-permute-done = bf16[3,2048]{0,1:T(8,128)(2,1)S(1)} collective-permute-done((bf16[3,2048]{0,1:T(8,128)(2,1)S(1)}, bf16[3,2048]{0,1:T(8,128)(2,1)S(1)}, u32[]{:S(2)}, u32[]{:S(2)}) %collective-permute-start) | collective-permute-done | bytes 12320 | tf_op jit(solution)/shard_map/ppermute | solution.py:19
  761.6 3.2 multiply_convert_fusion.2
  770.5 10.9 %all-gather = bf16[4,1,32]{2,1,0:T(2,128)(2,1)S(1)} all-gather(bf16[1,1,32]{2,1,0:T(2,128)(2,1)S(1)} %fusion.31), channel_id=1, replica_groups=mesh['groups'=2,'seq'=4,'tensor'=4] {'seq'}, dimensions={0}, use_global_device_ids=true | all-gather | bytes 320 | tf_op jit(solution)/shard_map/all_gather | solution.py:25
  784.6 2.8 multiply_convert_fusion
  787.4 28.9 %all-gather.13.cloned.1.call-done = bf16[4,32,64,128]{3,2,1,0:T(8,128)(2,1)} async-done(((bf16[1,32,64,128]{3,2,1,0:T(8,128)(2,1)}), bf16[4,32,64,128]{3,2,1,0:T(8,128)(2,1)}) %all-gather.13.cloned.1.call-update) | async-done | bytes 2097168 | tf_op jit(solution)/shard_map/all_gather | solution.py:25
  817.6 2.9 fusion.19
  821.7 4.2 fusion.11
  830.9 82.3 %all-gather.15.cloned.1.call-done = bf16[1024,2048]{0,1:T(8,128)(2,1)} async-done(((bf16[256,2048]{0,1:T(8,128)(2,1)}), bf16[1024,2048]{0,1:T(8,128)(2,1)}) %all-gather.15.cloned.1.call-update) | async-done | bytes 4194320 | tf_op jit(solution)/shard_map/all_gather | solution.py:193
  913.3 3.0 fusion.1
  916.7 5.8 convolution_convert_fusion
  924.4 6.8 all-reduce.2
  931.4 20.7 %reduce-scatter.2.cloned.1.call-done = bf16[256,1024]{1,0:T(8,128)(2,1)} async-done(((bf16[1024,1024]{1,0:T(8,128)(2,1)}), bf16[256,1024]{1,0:T(8,128)(2,1)}) %reduce-scatter.2.cloned.1.call-update) | async-done | bytes 524304 | tf_op jit(solution)/shard_map/reduce_scatter | solution.py:198
  (133 shorter events, 35.0 us)
Async XLA Ops:
  7.2 23.7 %copy-start = (bf16[256,4096]{1,0:T(8,128)(2,1)S(1)}, bf16[256,4096]{1,0:T(8,128)(2,1)}, u32[]{:S(2)}) copy-start(bf16[256,4096]{1,0:T(8,128)(2,1)} %param.19) | copy-start | bytes 6291460
  7.2 88.5 %all-gather.11.cloned.1.call-start = ((), (), s32[]{:S(2)}) async-start(), calls=%async_computation.3 | async-start | bytes 5242880 | tf_op jit(solution)/shard_map/all_gather | solution.py:109
  10.3 131.4 %all-gather.9.cloned.1.call-start = ((), (), s32[]{:S(2)}) async-start(), calls=%async_computation.2 | async-start | bytes 2621440 | tf_op jit(solution)/shard_map/all_gather | solution.py:111
  11.1 2.5 copy-start.14
  11.1 19.7 %copy-start.23 = (f32[32]{0:T(128)S(1)}, f32[32]{0:T(128)}, u32[]{:S(2)}) copy-start(f32[32]{0:T(128)} %param.30) | copy-start | bytes 388
  11.1 692.8 %all-gather.7.cloned.1.call-start = ((), (), s32[]{:S(2)}) async-start(), calls=%async_computation.1 | async-start | bytes 41943040 | tf_op jit(solution)/shard_map/all_gather | solution.py:108
  11.8 19.7 %copy-start.25 = (f32[16,32]{1,0:T(8,128)S(1)}, f32[16,32]{1,0:T(8,128)}, u32[]{:S(2)}) copy-start(f32[16,32]{1,0:T(8,128)} %param.31) | copy-start | bytes 6148
  11.9 19.7 %copy-start.26 = (s32[256]{0:T(256)S(1)}, s32[256]{0:T(256)}, u32[]{:S(2)}) copy-start(s32[256]{0:T(256)} %param.20) | copy-start | bytes 3076
  11.9 804.4 %all-gather.13.cloned.1.call-start = ((), (), s32[]{:S(2)}) async-start(), calls=%async_computation.4 | async-start | bytes 2621440 | tf_op jit(solution)/shard_map/all_gather | solution.py:25
  13.6 20.6 %copy-start.18 = (bf16[3,2048]{1,0:T(4,128)(2,1)S(1)}, bf16[3,2048]{1,0:T(4,128)(2,1)}, u32[]{:S(2)}) copy-start(bf16[3,2048]{1,0:T(4,128)(2,1)} %param.28) | copy-start | bytes 36868
  34.5 4.4 copy-start.17
  100.0 44.7 %collective-permute-start.1 = (bf16[3,512]{0,1:T(8,128)(2,1)S(1)}, bf16[3,512]{0,1:T(8,128)(2,1)S(1)}, u32[]{:S(2)}, u32[]{:S(2)}) collective-permute-start(bf16[3,512]{0,1:T(8,128)(2,1)S(1)} %slice.130), channel_id=1, source_target_pairs={{0,4},{4,8},{8,12},{1,5},{5,9},{9,13},{2,6},{6,10},{10,14},{3,7},{... | collective-permute-start | bytes 9224 | tf_op jit(solution)/shard_map/ppermute | solution.py:19
  727.1 15.2 %copy-start.6 = (bf16[32,8,2,2048]{3,1,2,0:T(8,128)(2,1)S(1)}, bf16[32,8,2,2048]{3,1,2,0:T(8,128)(2,1)}, u32[]{:S(2)}) copy-start(bf16[32,8,2,2048]{3,1,2,0:T(8,128)(2,1)} %copy.76) | copy-start | bytes 6291460
  727.1 15.2 %copy-start.11 = (bf16[256,256]{1,0:T(8,128)(2,1)S(1)}, bf16[256,256]{1,0:T(8,128)(2,1)}, u32[]{:S(2)}) copy-start(bf16[256,256]{1,0:T(8,128)(2,1)} %fusion.17) | copy-start | bytes 393220
  747.7 13.2 %copy-start.3 = (bf16[256,4096]{0,1:T(8,128)(2,1)}, bf16[256,4096]{0,1:T(8,128)(2,1)S(1)}, u32[]{:S(2)}) copy-start(bf16[256,4096]{0,1:T(8,128)(2,1)S(1)} %copy.71) | copy-start | bytes 6291460
  747.9 12.9 %collective-permute-start = (bf16[3,2048]{0,1:T(8,128)(2,1)S(1)}, bf16[3,2048]{0,1:T(8,128)(2,1)S(1)}, u32[]{:S(2)}, u32[]{:S(2)}) collective-permute-start(bf16[3,2048]{0,1:T(8,128)(2,1)S(1)} %slice_bitcast_fusion.2), channel_id=1, source_target_pairs={{0,4},{4,8},{8,12},{1,5},{5,9},{9,13},{2,6},{6,10},{10,14},{3,7},{... | collective-permute-start | bytes 36872 | tf_op jit(solution)/shard_map/ppermute | solution.py:19
  767.9 13.5 %copy-start.9 = (f32[2,128,32]{2,1,0:T(8,128)S(1)}, f32[2,128,32]{2,1,0:T(8,128)}, u32[]{:S(2)}) copy-start(f32[2,128,32]{2,1,0:T(8,128)} %get-tuple-element.60) | copy-start | bytes 98308
  769.7 143.5 %all-gather.15.cloned.1.call-start = ((), (), s32[]{:S(2)}) async-start(), calls=%async_computation.5 | async-start | bytes 5242880 | tf_op jit(solution)/shard_map/all_gather | solution.py:193
  821.7 4.2 copy-start.5
  821.7 4.2 copy-start.12
  829.2 84.1 %copy-start.19 = (f32[2048]{0:T(1024)S(1)}, f32[2048]{0:T(1024)}, u32[]{:S(2)}) copy-start(f32[2048]{0:T(1024)} %param.34) | copy-start | bytes 24580
  830.9 121.2 %reduce-scatter.2.cloned.1.call-start = ((), (), s32[]{:S(2)}) async-start(), calls=%async_computation.6 | async-start | bytes 2621440 | tf_op jit(solution)/shard_map/reduce_scatter | solution.py:198
  913.3 3.4 copy-start.24
  916.7 37.3 %copy-start.1 = (bf16[256,4096]{1,0:T(8,128)(2,1)S(1)}, bf16[256,4096]{1,0:T(8,128)(2,1)}, u32[]{:S(2)}) copy-start(bf16[256,4096]{1,0:T(8,128)(2,1)} %param.19) | copy-start | bytes 6291460
  (13 other events, 13.0 us)
Sparse Core Ops, SparseCore 0:
  10.4 85.1 all-gather.10
  97.2 44.4 all-gather.8
  143.3 560.5 all-gather.6
  769.7 46.5 all-gather.12
  831.0 82.2 all-gather.14
  922.7 29.3 reduce-scatter.1
where the time goes:
time: 962 us; the launch traced here: 961 us
  waiting for transfers between devices  799 us (83%)
  local copies, waits for them, and re-layouts  52.5 us (5%)
  matrix products  35 us (4%)
  blocking collectives  34.9 us (4%)
  other arithmetic  21.6 us (2%)
  between operations  15.3 us (2%)
    all_gather x1, waiting for transfers between devices, per_device(): lax.all_gather(gate_scanned_weight, 'seq', axis=0, tiled=True)  557 us
    all_gather x1, waiting for transfers between devices, per_device(): gathered = lax.all_gather(gated, 'seq', axis=0, tiled=True)  82.3 us
    all_gather x1, waiting for transfers between devices, per_device(): lax.all_gather(mine_io, 'seq', axis=0, tiled=True)  56.1 us
    all_gather x1, waiting for transfers between devices, per_device(): lax.all_gather(adapter_down_maps, 'seq', axis=0, tiled=True)  40.3 us
    unnamed x71, local copies, waits for them, and re-layouts  37 us
    all_gather x1, waiting for transfers between devices, entering_2(): lax.all_gather(a.astype(kind), axis)  28.9 us
    reduce_scatter x1, waiting for transfers between devices, per_device(): lax.psum_scatter(partial_sum.astype(jnp.bfloat16), 'tensor', scatter_dime...  20.7 us
    dot_general x4, matrix products, add_product(): jnp.dot(activations, piece.reshape(piece.shape[0], -1), preferred_element...  20.2 us
  transfers between devices with their start and end apart: 8, of which 7 were waited for; matrix products, arithmetic and copies ran while one was open for 3% of the time, Pallas kernels for 0%

commit v1 on v0

--- a/solution.py
+++ b/solution.py
@@ -11,6 +11,16 @@
 ADAPTER_RANK = 16
 CONV = 4
 BLOCK = 128
+
+
+def ring_gather(x, axis, dim):
+    ways, here, lap = (lax.axis_size(axis), lax.axis_index(axis), x.shape[dim])
+    lengths = [n * ways if d == dim else n for d, n in enumerate(x.shape)]
+    full = lax.dynamic_update_slice_in_dim(jnp.zeros(lengths, x.dtype), x, here * lap, axis=dim)
+    for far in range(1, ways):
+        x = lax.ppermute(x, axis, [(d, (d + 1) % ways) for d in range(ways)])
+        full = lax.dynamic_update_slice_in_dim(full, x, (here - far) % ways * lap, axis=dim)
+    return full
 
 
 def passed_along(array, axis, by):
@@ -106,7 +116,7 @@
 
     pieces = (
         lax.all_gather(gate_scanned_weight, "seq", axis=0, tiled=True),
-        lax.all_gather(mine_io, "seq", axis=0, tiled=True),
+        ring_gather(mine_io, "seq", 0),
         lax.all_gather(time_step_weight, "seq", axis=0, tiled=True),
         lax.all_gather(adapter_down_maps, "seq", axis=0, tiled=True),
     )

time: 962 us -> 931 us (0.968)
  waiting for transfers between devices: 799 us -> 670 us
  blocking collectives: 34.9 us -> 96.1 us
  starting transfers between devices: 3 us -> 24.6 us
  local copies, waits for them, and re-layouts: 52.5 us -> 67.2 us
    all_gather x1, waiting for transfers between devices: 557 us -> 438 us  [per_device(): lax.all_gather(gate_scanned_weight, 'seq', axis=0, tiled=True)]
    ppermute x0 -> x3, waiting for transfers between devices: none -> 84.8 us  [ring_gather(): x = lax.ppermute(x, axis, [(d, (d + 1) % ways) for d in range(ways)])]
    all_gather x1, blocking collectives: 17.2 us -> 76 us  [per_device(): lax.all_gather(time_step_weight, 'seq', axis=0, tiled=True)]
    all_gather x1 -> x0, waiting for transfers between devices: 56.1 us -> none  [per_device(): lax.all_gather(mine_io, 'seq', axis=0, tiled=True)]
    all_gather x1, waiting for transfers between devices: 40.3 us -> 0.02 us  [per_device(): lax.all_gather(adapter_down_maps, 'seq', axis=0, tiled=True)]
    ppermute x0 -> x3, starting transfers between devices: none -> 14.2 us  [ring_gather(): x = lax.ppermute(x, axis, [(d, (d + 1) % ways) for d in range(ways)])]
    dynamic_update_slice x0 -> x4, local copies, waits for them, and re-layouts: none -> 10.9 us  [the longest x3 7.55 us: ring_gather(): lax.dynamic_update_slice_in_dim(full, x, (here - far) % ways * lap, axis=...]
    unnamed x71 -> x69, local copies, waits for them, and re-layouts: 37 us -> 39.3 us
  transfers between devices with their start and end apart: 8 -> 10, of which waited for: 7 -> 8; matrix products, arithmetic and copies ran while one was open for 3% -> 5% of each run, Pallas kernels for 0% -> 0%
where the time goes in v1:
time: 931 us; the launch traced here: 930 us
  waiting for transfers between devices  670 us (72%)
  blocking collectives  96.1 us (10%)
  local copies, waits for them, and re-layouts  67.2 us (7%)
  matrix products  34.4 us (4%)
  starting transfers between devices  24.6 us (3%)
  other arithmetic  22.8 us (2%)
  between operations  15 us (2%)
    all_gather x1, waiting for transfers between devices, per_device(): lax.all_gather(gate_scanned_weight, 'seq', axis=0, tiled=True)  438 us
    ppermute x3, waiting for transfers between devices, ring_gather(): x = lax.ppermute(x, axis, [(d, (d + 1) % ways) for d in range(ways)])  84.8 us
    all_gather x1, waiting for transfers between devices, per_device(): gathered = lax.all_gather(gated, 'seq', axis=0, tiled=True)  82.3 us
    all_gather x1, blocking collectives, per_device(): lax.all_gather(time_step_weight, 'seq', axis=0, tiled=True)  76 us
    unnamed x69, local copies, waits for them, and re-layouts  39.3 us
    all_gather x1, waiting for transfers between devices, entering_2(): lax.all_gather(a.astype(kind), axis)  28.6 us
    reduce_scatter x1, waiting for transfers between devices, per_device(): lax.psum_scatter(partial_sum.astype(jnp.bfloat16), 'tensor', scatter_dime...  20.7 us
    dot_general x4, matrix products, add_product(): jnp.dot(activations, piece.reshape(piece.shape[0], -1), preferred_element...  19.6 us
  transfers between devices with their start and end apart: 10, of which 8 were waited for; matrix products, arithmetic and copies ran while one was open for 5% of the time, Pallas kernels for 0%

profile of v1, /device:TPU:0, one launch (start us, length us, event | category | flops | bytes accessed | tf_op | source)
XLA Modules:
  0.0 930.4 jit_solution(3200092755047495365)
XLA Ops:
  8.7 4.6 broadcast_in_dim.28
  13.3 3.3 constant_dynamic-update-slice_fusion.3
  16.7 3.0 collective-permute-start.1
  23.6 42.6 %collective-permute-done.1 = bf16[1024,2,256]{2,1,0:T(2,128)(2,1)} collective-permute-done((bf16[1024,2,256]{2,1,0:T(2,128)(2,1)S(1)}, bf16[1024,2,256]{2,1,0:T(2,128)(2,1)}, u32[]{:S(2)}, u32[]{:S(2)}) %collective-permute-start.1) | collective-permute-done | bytes 1048608 | tf_op jit(solution)/shard_map/ppermute | solution.py:21
  66.3 11.2 %collective-permute-start.2 = (bf16[1024,2,256]{2,1,0:T(2,128)(2,1)}, bf16[1024,2,256]{2,1,0:T(2,128)(2,1)}, u32[]{:S(2)}, u32[]{:S(2)}) collective-permute-start(bf16[1024,2,256]{2,1,0:T(2,128)(2,1)} %collective-permute-done.1), channel_id=1, source_target_pairs={{0,4},{4,8},{8,12},{12,0},{1,5},{5,9},{9,13},{13,1},{2,6},{6,10},{... | collective-permute-start | bytes 3145736 | tf_op jit(solution)/shard_map/ppermute | solution.py:21
  77.4 76.0 %all_gather.22 = bf16[4096,32]{0,1:T(8,128)(2,1)S(1)} all-gather(bf16[1024,32]{0,1:T(8,128)(2,1)S(1)} %copy-done.13), channel_id=1, replica_groups=mesh['groups'=2,'seq'=4,'tensor'=4] {'seq'}, dimensions={0}, use_global_device_ids=true | all-gather | bytes 327680 | tf_op jit(solution)/shard_map/all_gather | solution.py:120
  157.2 3.9 copy.76
  168.7 42.2 %collective-permute-done.3 = bf16[1024,2,256]{2,1,0:T(2,128)(2,1)S(1)} collective-permute-done((bf16[1024,2,256]{2,1,0:T(2,128)(2,1)}, bf16[1024,2,256]{2,1,0:T(2,128)(2,1)S(1)}, u32[]{:S(2)}, u32[]{:S(2)}) %collective-permute-start.3) | collective-permute-done | bytes 1048608 | tf_op jit(solution)/shard_map/ppermute | solution.py:21
  216.9 7.0 collective-permute-start.4
  231.7 438.2 %all-gather.6.cloned.1.call-done = bf16[4096,2,2048]{2,1,0:T(2,128)(2,1)} async-done(((bf16[1024,2,2048]{2,1,0:T(2,128)(2,1)}), bf16[4096,2,2048]{2,1,0:T(2,128)(2,1)}) %all-gather.6.cloned.1.call-update) | async-done | bytes 33554448 | tf_op jit(solution)/shard_map/all_gather | solution.py:118
  669.9 23.2 %copy.75 = bf16[512,8,2,2048]{3,1,2,0:T(8,128)(2,1)} copy(bf16[512,8,2,2048]{3,2,1,0:T(2,128)(2,1)} %bitcast.126) | data formatting | bytes 67108864
  693.1 15.2 %fusion.43 = f32[256,4096]{1,0:T(8,128)S(1)} fusion(bf16[256,4096]{1,0:T(8,128)(2,1)S(1)} %copy-done, bf16[4096,4096]{1,0:T(8,128)(2,1)} %bitcast.127), kind=kOutput, calls=%fused_computation.110 | convolution fusion | flops 8589934592 | bytes 39845888 | tf_op jit(solution)/shard_map/dot_general | solution.py:113
  710.4 3.3 copy.71
  713.9 3.2 collective-permute-start
  717.2 11.3 %collective-permute-done = bf16[3,2048]{0,1:T(8,128)(2,1)S(1)} collective-permute-done((bf16[3,2048]{0,1:T(8,128)(2,1)S(1)}, bf16[3,2048]{0,1:T(8,128)(2,1)S(1)}, u32[]{:S(2)}, u32[]{:S(2)}) %collective-permute-start) | collective-permute-done | bytes 12320 | tf_op jit(solution)/shard_map/ppermute | solution.py:29
  729.3 3.2 multiply_convert_fusion.2
  738.2 13.2 %all-gather = bf16[4,1,32]{2,1,0:T(2,128)(2,1)S(1)} all-gather(bf16[1,1,32]{2,1,0:T(2,128)(2,1)S(1)} %fusion.35), channel_id=1, replica_groups=mesh['groups'=2,'seq'=4,'tensor'=4] {'seq'}, dimensions={0}, use_global_device_ids=true | all-gather | bytes 320 | tf_op jit(solution)/shard_map/all_gather | solution.py:35
  757.5 28.6 %all-gather.10.cloned.1.call-done = bf16[4,32,64,128]{3,2,1,0:T(8,128)(2,1)} async-done(((bf16[1,32,64,128]{3,2,1,0:T(8,128)(2,1)}), bf16[4,32,64,128]{3,2,1,0:T(8,128)(2,1)}) %all-gather.10.cloned.1.call-update) | async-done | bytes 2097168 | tf_op jit(solution)/shard_map/all_gather | solution.py:35
  791.6 4.2 fusion.11
  800.8 82.3 %all-gather.12.cloned.1.call-done = bf16[1024,2048]{0,1:T(8,128)(2,1)} async-done(((bf16[256,2048]{0,1:T(8,128)(2,1)}), bf16[1024,2048]{0,1:T(8,128)(2,1)}) %all-gather.12.cloned.1.call-update) | async-done | bytes 4194320 | tf_op jit(solution)/shard_map/all_gather | solution.py:203
  883.1 3.0 fusion.1
  886.6 5.8 convolution_convert_fusion
  894.3 6.8 all-reduce.2
  901.2 20.7 %reduce-scatter.2.cloned.1.call-done = bf16[256,1024]{1,0:T(8,128)(2,1)} async-done(((bf16[1024,1024]{1,0:T(8,128)(2,1)}), bf16[256,1024]{1,0:T(8,128)(2,1)}) %reduce-scatter.2.cloned.1.call-update) | async-done | bytes 524304 | tf_op jit(solution)/shard_map/reduce_scatter | solution.py:208
  (138 shorter events, 59.3 us)
Async XLA Ops:
  7.2 146.3 %copy-start = (bf16[256,4096]{1,0:T(8,128)(2,1)S(1)}, bf16[256,4096]{1,0:T(8,128)(2,1)}, u32[]{:S(2)}) copy-start(bf16[256,4096]{1,0:T(8,128)(2,1)} %param.19) | copy-start | bytes 6291460
  7.2 216.8 %all-gather.8.cloned.1.call-start = ((), (), s32[]{:S(2)}) async-start(), calls=%async_computation.2 | async-start | bytes 2621440 | tf_op jit(solution)/shard_map/all_gather | solution.py:121
  7.9 662.0 %all-gather.6.cloned.1.call-start = ((), (), s32[]{:S(2)}) async-start(), calls=%async_computation.1 | async-start | bytes 41943040 | tf_op jit(solution)/shard_map/all_gather | solution.py:118
  8.7 777.4 %all-gather.10.cloned.1.call-start = ((), (), s32[]{:S(2)}) async-start(), calls=%async_computation.3 | async-start | bytes 2621440 | tf_op jit(solution)/shard_map/all_gather | solution.py:35
  13.3 6.4 copy-start.26
  13.3 64.1 %copy-start.13 = (bf16[1024,32]{0,1:T(8,128)(2,1)S(1)}, bf16[1024,32]{0,1:T(8,128)(2,1)}, u32[]{:S(2)}) copy-start(bf16[1024,32]{0,1:T(8,128)(2,1)} %param.23) | copy-start | bytes 196612
  13.3 140.1 %copy-start.22 = (f32[32]{0:T(128)S(1)}, f32[32]{0:T(128)}, u32[]{:S(2)}) copy-start(f32[32]{0:T(128)} %param.30) | copy-start | bytes 388
  16.7 137.5 %copy-start.24 = (f32[16,32]{1,0:T(8,128)S(1)}, f32[16,32]{1,0:T(8,128)}, u32[]{:S(2)}) copy-start(f32[16,32]{1,0:T(8,128)} %param.31) | copy-start | bytes 6148
  16.7 137.5 %copy-start.25 = (s32[256]{0:T(256)S(1)}, s32[256]{0:T(256)}, u32[]{:S(2)}) copy-start(s32[256]{0:T(256)} %param.20) | copy-start | bytes 3076
  16.7 49.6 %collective-permute-start.1 = (bf16[1024,2,256]{2,1,0:T(2,128)(2,1)S(1)}, bf16[1024,2,256]{2,1,0:T(2,128)(2,1)}, u32[]{:S(2)}, u32[]{:S(2)}) collective-permute-start(bf16[1024,2,256]{2,1,0:T(2,128)(2,1)S(1)} %get-tuple-element.55), channel_id=1, source_target_pairs={{0,4},{4,8},{8,12},{12,0},{1,5},{5,9},{9,13},{13,1},{2,6},{6,10},{... | collective-permute-start | bytes 3145736 | tf_op jit(solution)/shard_map/ppermute | solution.py:21
  23.6 133.2 %copy-start.17 = (bf16[3,2048]{1,0:T(4,128)(2,1)S(1)}, bf16[3,2048]{1,0:T(4,128)(2,1)}, u32[]{:S(2)}) copy-start(bf16[3,2048]{1,0:T(4,128)(2,1)} %param.28) | copy-start | bytes 36868
  66.3 94.8 %collective-permute-start.2 = (bf16[1024,2,256]{2,1,0:T(2,128)(2,1)}, bf16[1024,2,256]{2,1,0:T(2,128)(2,1)}, u32[]{:S(2)}, u32[]{:S(2)}) collective-permute-start(bf16[1024,2,256]{2,1,0:T(2,128)(2,1)} %collective-permute-done.1), channel_id=1, source_target_pairs={{0,4},{4,8},{8,12},{12,0},{1,5},{5,9},{9,13},{13,1},{2,6},{6,10},{... | collective-permute-start | bytes 3145736 | tf_op jit(solution)/shard_map/ppermute | solution.py:21
  157.1 5.0 copy-start.16
  161.0 49.9 %collective-permute-start.3 = (bf16[1024,2,256]{2,1,0:T(2,128)(2,1)}, bf16[1024,2,256]{2,1,0:T(2,128)(2,1)S(1)}, u32[]{:S(2)}, u32[]{:S(2)}) collective-permute-start(bf16[1024,2,256]{2,1,0:T(2,128)(2,1)} %collective-permute-done.2), channel_id=1, source_target_pairs={{0,4},{4,8},{8,12},{12,0},{1,5},{5,9},{9,13},{13,1},{2,6},{6,10},{... | collective-permute-start | bytes 3145736 | tf_op jit(solution)/shard_map/ppermute | solution.py:21
  216.9 12.2 %collective-permute-start.4 = (bf16[3,512]{0,1:T(8,128)(2,1)S(1)}, bf16[3,512]{0,1:T(8,128)(2,1)S(1)}, u32[]{:S(2)}, u32[]{:S(2)}) collective-permute-start(bf16[3,512]{0,1:T(8,128)(2,1)S(1)} %slice.130), channel_id=1, source_target_pairs={{0,4},{4,8},{8,12},{1,5},{5,9},{9,13},{2,6},{6,10},{10,14},{3,7},{... | collective-permute-start | bytes 9224 | tf_op jit(solution)/shard_map/ppermute | solution.py:29
  693.1 15.2 %copy-start.6 = (bf16[32,8,2,2048]{3,1,2,0:T(8,128)(2,1)S(1)}, bf16[32,8,2,2048]{3,1,2,0:T(8,128)(2,1)}, u32[]{:S(2)}) copy-start(bf16[32,8,2,2048]{3,1,2,0:T(8,128)(2,1)} %copy.76) | copy-start | bytes 6291460
  713.7 14.9 %copy-start.3 = (bf16[256,4096]{0,1:T(8,128)(2,1)}, bf16[256,4096]{0,1:T(8,128)(2,1)S(1)}, u32[]{:S(2)}) copy-start(bf16[256,4096]{0,1:T(8,128)(2,1)S(1)} %copy.71) | copy-start | bytes 6291460
  713.9 14.6 %collective-permute-start = (bf16[3,2048]{0,1:T(8,128)(2,1)S(1)}, bf16[3,2048]{0,1:T(8,128)(2,1)S(1)}, u32[]{:S(2)}, u32[]{:S(2)}) collective-permute-start(bf16[3,2048]{0,1:T(8,128)(2,1)S(1)} %slice_bitcast_fusion.2), channel_id=1, source_target_pairs={{0,4},{4,8},{8,12},{1,5},{5,9},{9,13},{2,6},{6,10},{10,14},{3,7},{... | collective-permute-start | bytes 36872 | tf_op jit(solution)/shard_map/ppermute | solution.py:29
  735.6 15.9 %copy-start.9 = (f32[2,128,32]{2,1,0:T(8,128)S(1)}, f32[2,128,32]{2,1,0:T(8,128)}, u32[]{:S(2)}) copy-start(f32[2,128,32]{2,1,0:T(8,128)} %get-tuple-element.62) | copy-start | bytes 98308
  737.4 145.7 %all-gather.12.cloned.1.call-start = ((), (), s32[]{:S(2)}) async-start(), calls=%async_computation.4 | async-start | bytes 5242880 | tf_op jit(solution)/shard_map/all_gather | solution.py:203
  791.6 4.2 copy-start.12
  799.0 84.1 %copy-start.18 = (f32[2048]{0:T(1024)S(1)}, f32[2048]{0:T(1024)}, u32[]{:S(2)}) copy-start(f32[2048]{0:T(1024)} %param.34) | copy-start | bytes 24580
  800.7 121.2 %reduce-scatter.2.cloned.1.call-start = ((), (), s32[]{:S(2)}) async-start(), calls=%async_computation.5 | async-start | bytes 2621440 | tf_op jit(solution)/shard_map/reduce_scatter | solution.py:208
  886.6 37.3 %copy-start.1 = (bf16[256,4096]{1,0:T(8,128)(2,1)S(1)}, bf16[256,4096]{1,0:T(8,128)(2,1)}, u32[]{:S(2)}) copy-start(bf16[256,4096]{1,0:T(8,128)(2,1)} %param.19) | copy-start | bytes 6291460
  (14 other events, 19.8 us)
Sparse Core Ops, SparseCore 0:
  9.6 69.5 all-gather.7
  80.7 589.1 all-gather.5
  737.4 48.6 all-gather.9
  800.8 82.2 all-gather.11
  892.5 29.3 reduce-scatter.1
